TPU v7x, 512 devices: a whole 4x4x16 slice. The times are simulated.
512 devices in a mesh: expert: 32 (over z, core), dp: 16 (over x, y).
Axes of the slice: x: 4, y: 4, z: 16, core: 2. Of those that a mesh axis runs over, the one named last changes fastest.
Arguments:
- patches: bfloat16 [16, 32, 128, 1664], P('dp', 'expert'), may hold values from -6 to 6
- grad_out: bfloat16 [16, 32, 128, 1664], P('dp', 'expert'), may hold values from -3 to 3
- weight_in: bfloat16 [32, 1664, 4096], P('expert', None, 'dp'), may hold values from -0.15625 to 0.15625
- weight_out: bfloat16 [32, 4096, 1664], P('expert', 'dp'), may hold values from -0.09375 to 0.09375
- gates: float32 [32, 16, 32], P('expert', 'dp'), may hold values from 0.1 to 1
- counts: int32 [16, 32, 32], P(None, None, 'expert'), may hold values from 0 to 2, as said below
- picks: int32 [16, 32, 32, 2], P('dp', 'expert'), may hold values from 0 to 127, as said below
Outputs:
- grad_patches: bfloat16 [16, 32, 128, 1664], P('dp', 'expert')
- grad_weight_in: bfloat16 [32, 1664, 4096], P('expert', None, 'dp')
- grad_weight_out: bfloat16 [32, 4096, 1664], P('expert', 'dp')
Inputs may be any that keep to these rules, and one draw needn't show every extreme that they name: For each group and expert the counts over the 32 owner blocks sum to exactly 32, and in every group each expert takes 2 patches from some owner block. `picks`: for each group, owner block and expert the entries are distinct; only the first counts[g, o, e] of them are taken, the rest are arbitrary patch indices of the block.
All inputs are finite; a program needn't handle non-finite values.
Results may differ from a plain program's by a relative error of at most 0.015.
Values may be sent and summed in bfloat16 or wider, within the bound.
A program may use at most 64 MiB of HBM per device.

v0:
```python
import jax
import jax.numpy as jnp
from jax import lax
from jax.sharding import PartitionSpec as P

gelu_scale = 0.7978845608028654
gelu_cubic = 0.044715


def gelu_parts(preact):
    inner_arg = gelu_scale * (preact + gelu_cubic * preact * preact * preact)
    tangent = jnp.tanh(inner_arg)
    gelu_value = 0.5 * preact * (1.0 + tangent)
    gelu_slope = 0.5 * (1.0 + tangent) + 0.5 * preact * (1.0 - tangent * tangent) * gelu_scale * (
        1.0 + 3.0 * gelu_cubic * preact * preact
    )
    return (gelu_value, gelu_slope)


def slot_tables(owner_counts, capacity):
    owners = owner_counts.shape[-1]
    slot_ends = jnp.cumsum(owner_counts, axis=-1)
    begins = slot_ends - owner_counts
    slot_ids = jnp.arange(capacity, dtype=jnp.int32)
    owner_of = jnp.sum((slot_ends[..., None, :] <= slot_ids[:, None]).astype(jnp.int32), axis=-1)
    matches = owner_of[..., None] == jnp.arange(owners, dtype=jnp.int32)
    rank_in = slot_ids - jnp.sum(jnp.where(matches, begins[..., None, :], 0), axis=-1)
    return (owner_of, rank_in)


def on_device(patches, grad_out, weight_in, weight_out, gates, counts, picks):
    tok_local = patches.shape[2]
    dim_model = patches.shape[3]
    experts = picks.shape[2]
    per_owner = picks.shape[3]
    groups = counts.shape[0]
    owners = counts.shape[1]
    capacity = gates.shape[2]
    local_in = weight_in[0]
    local_out = weight_out[0]
    chosen = picks[0, 0].reshape(experts * per_owner)
    send_in = jnp.take(patches[0, 0], chosen, axis=0).reshape(experts, per_owner, dim_model)
    send_grad = jnp.take(grad_out[0, 0], chosen, axis=0).reshape(experts, per_owner, dim_model)
    arrived_in, arrived_grad = (
        lax.all_to_all(send_in, "expert", split_axis=0, concat_axis=0, tiled=True),
        lax.all_to_all(send_grad, "expert", split_axis=0, concat_axis=0, tiled=True),
    )
    arrived_in = arrived_in.reshape(owners * per_owner, dim_model)
    arrived_grad = arrived_grad.reshape(owners * per_owner, dim_model)
    all_counts = counts[:, :, 0]
    group_index = lax.axis_index("dp")
    my_counts = lax.dynamic_index_in_dim(all_counts, group_index, 0, keepdims=False)
    my_begins = jnp.cumsum(my_counts) - my_counts
    rank_ids = jnp.arange(per_owner, dtype=jnp.int32)
    slot_of = (my_begins[:, None] + rank_ids[None, :]).reshape(owners * per_owner)
    is_valid = (rank_ids[None, :] < my_counts[:, None]).reshape(owners * per_owner)
    my_gates = gates[0, 0]
    slot_hits = (slot_of[:, None] == jnp.arange(capacity, dtype=jnp.int32)[None, :]) & is_valid[
        :, None
    ]
    padded_gates = jnp.sum(jnp.where(slot_hits, my_gates[None, :], 0.0), axis=1)
    scaled_rows = (padded_gates[:, None] * arrived_grad.astype(jnp.float32)).astype(jnp.bfloat16)
    piece_in = lax.all_gather(arrived_in, "dp", axis=0, tiled=True)
    piece_grad = lax.all_gather(scaled_rows, "dp", axis=0, tiled=True)
    preact = jnp.dot(piece_in, local_in, preferred_element_type=jnp.float32)
    gelu_value, gelu_slope = gelu_parts(preact)
    hidden = gelu_value.astype(jnp.bfloat16)
    grad_hidden = lax.dot_general(
        piece_grad, local_out, (((1,), (1,)), ((), ())), preferred_element_type=jnp.float32
    )
    grad_pre = (grad_hidden * gelu_slope).astype(jnp.bfloat16)
    sum_out = lax.dot_general(
        hidden, piece_grad, (((0,), (0,)), ((), ())), preferred_element_type=jnp.float32
    )
    sum_in = lax.dot_general(
        piece_in, grad_pre, (((0,), (0,)), ((), ())), preferred_element_type=jnp.float32
    )
    sum_in, sum_out, grad_stash = (sum_in, sum_out, grad_pre)
    owner_all, rank_all = slot_tables(all_counts, capacity)
    group_base = jnp.arange(groups, dtype=jnp.int32)[:, None] * (owners * per_owner)
    padded_index = (group_base + owner_all * per_owner + rank_all).reshape(groups * capacity)
    stash_rows = jnp.take(grad_stash, padded_index, axis=0)
    expert_grad = lax.psum_scatter(
        lax.dot_general(
            stash_rows, local_in, (((1,), (1,)), ((), ())), preferred_element_type=jnp.float32
        ).astype(jnp.bfloat16),
        "dp",
        scatter_dimension=0,
        tiled=True,
    )
    returned = jnp.take(expert_grad, jnp.clip(slot_of, 0, capacity - 1), axis=0)
    returned = jnp.where(is_valid[:, None], returned, jnp.zeros_like(returned))
    returned = returned.reshape(owners, per_owner, dim_model)
    arrived_back = lax.all_to_all(returned, "expert", split_axis=0, concat_axis=0, tiled=True)
    arrived_back = arrived_back.reshape(experts * per_owner, dim_model)
    owner_table = (jnp.arange(tok_local, dtype=jnp.int32)[:, None] == chosen[None, :]).astype(
        jnp.bfloat16
    )
    grad_local = jnp.dot(owner_table, arrived_back, preferred_element_type=jnp.float32).astype(
        jnp.bfloat16
    )
    return (
        grad_local[None, None],
        sum_in.astype(jnp.bfloat16)[None],
        sum_out.astype(jnp.bfloat16)[None],
    )


def solution(mesh):
    return jax.shard_map(
        on_device,
        mesh=mesh,
        in_specs=(
            P("dp", "expert", None, None),
            P("dp", "expert", None, None),
            P("expert", None, "dp"),
            P("expert", "dp", None),
            P("expert", "dp", None),
            P(None, None, "expert"),
            P("dp", "expert", None, None),
        ),
        out_specs=(P("dp", "expert", None, None), P("expert", None, "dp"), P("expert", "dp", None)),
        check_vma=False,
    )
```

profile of v0, /device:TPU:1, one launch (start us, length us, event | category | flops | bytes accessed | tf_op | source)
XLA Modules:
  0.0 311.9 jit_solution(8683857423019029709)
XLA Ops:
  7.2 0.0 copy-start
  7.2 0.0 all-gather.5.cloned.1.call-start
  7.2 0.8 copy.14
  8.1 0.1 eq.42
  8.2 0.0 copy-start.1
  8.2 0.0 copy-start.2
  8.2 2.0 gather_fusion.3
  10.2 2.0 gather_fusion.2
  12.2 0.1 broadcast_select_fusion.2
  12.3 0.1 reshape.235
  12.4 36.1 %all_to_all.15 = bf16[32,2,1664]{2,1,0:T(2,128)(2,1)S(1)} all-to-all(bf16[32,2,1664]{2,1,0:T(2,128)(2,1)S(1)} %reshape.235), channel_id=1, replica_groups=mesh['expert'=32,'dp'=16] {'expert'}, dimensions={0} | all-to-all | bytes 425984 | tf_op jit(solution)/shard_map/all_to_all | solution.py:45
  48.6 0.8 reshape.236
  49.3 0.0 all-gather.5.cloned.1.call-update
  49.3 0.8 reshape.234
  50.1 4.9 %all-to-all-start = ((bf16[32,2,1664]{2,1,0:T(2,128)(2,1)}), bf16[32,2,1664]{2,1,0:T(2,128)(2,1)S(1)}, u32[]{:S(2)}, u32[]{:S(2)}) async-start(bf16[32,2,1664]{2,1,0:T(2,128)(2,1)} %reshape.234), calls=%async_computation | async-start | bytes 425984 | tf_op jit(solution)/shard_map/all_to_all | solution.py:46
  55.0 0.0 all-gather.3.cloned.1.call-start
  55.0 0.0 copy-done.1
  55.1 0.1 copy.15
  55.2 0.1 reduce-window.8
  55.2 0.1 reduce
  55.3 0.1 iota_compare_fusion.5
  55.4 0.1 lt.83
  55.5 0.1 broadcast_clamp_fusion
  55.6 0.1 add.147
  55.7 0.0 copy-done.2
  55.7 0.1 select_reduce_fusion.1
  55.8 18.8 %all-to-all-done = bf16[32,2,1664]{2,1,0:T(2,128)(2,1)S(1)} async-done(((bf16[32,2,1664]{2,1,0:T(2,128)(2,1)}), bf16[32,2,1664]{2,1,0:T(2,128)(2,1)S(1)}, u32[]{:S(2)}, u32[]{:S(2)}) %all-to-all-start) | async-done | bytes 213024 | tf_op jit(solution)/shard_map/all_to_all | solution.py:46
  74.6 0.1 reshape.238
  74.7 0.8 multiply_convert_fusion.2
  75.5 0.0 all-gather.3.cloned.1.call-update
  75.5 0.0 reduce-scatter.2.cloned.1.call-start
  75.5 0.2 reduce_window_sum.18
  75.7 0.3 convert_reduce_fusion
  76.1 0.5 select_reduce_fusion
  76.5 0.1 subtract_add_fusion
  76.6 0.1 add.152
  76.7 0.1 add.144
  76.8 0.0 copy-start.4
  76.8 28.1 %all-gather.5.cloned.1.call-done = bf16[1024,1664]{1,0:T(8,128)(2,1)} async-done(((bf16[64,1664]{1,0:T(8,128)(2,1)}), bf16[1024,1664]{1,0:T(8,128)(2,1)}) %all-gather.5.cloned.1.call-update) | async-done | bytes 3407888 | tf_op jit(solution)/shard_map/all_gather | solution.py:63
  104.9 0.0 copy-done
  104.9 3.1 fusion.10
  108.0 63.5 %all-gather.3.cloned.1.call-done = bf16[1024,1664]{1,0:T(8,128)(2,1)} async-done(((bf16[64,1664]{1,0:T(8,128)(2,1)}), bf16[1024,1664]{1,0:T(8,128)(2,1)}) %all-gather.3.cloned.1.call-update) | async-done | bytes 3407888 | tf_op jit(solution)/shard_map/all_gather | solution.py:64
  171.5 0.0 copy-done.4
  171.5 3.5 %fusion.3 = bf16[1024,256]{1,0:T(8,128)(2,1)S(1)} fusion(bf16[1024,1664]{1,0:T(8,128)(2,1)} %all-gather.3.cloned.1.call-done, f32[1024,256]{1,0:T(8,128)S(1)} %fusion.10, bf16[1,256,1664]{2,1,0:T(8,128)(2,1)S(1)} %copy-done.4), kind=kOutput, calls=%fused_computation.14 | convolution fusion | flops 877395968 | bytes 5832704 | tf_op jit(solution)/shard_map/dot_general | solution.py:68
  174.9 2.0 gather_fusion
  176.9 1.9 convolution_convert_fusion
  178.8 0.0 reduce-scatter.2.cloned.1.call-update
  178.8 0.1 min.12
  179.0 0.1 compare_and_fusion
  179.0 87.9 %reduce-scatter.2.cloned.1.call-done = bf16[32,1664]{1,0:T(8,128)(2,1)} async-done(((bf16[512,1664]{1,0:T(8,128)(2,1)}), bf16[32,1664]{1,0:T(8,128)(2,1)}) %reduce-scatter.2.cloned.1.call-update) | async-done | bytes 106512 | tf_op jit(solution)/shard_map/reduce_scatter | solution.py:83
  267.0 1.8 gather_fusion.1
  268.8 0.1 gather.15
  268.9 1.1 broadcast_select_fusion.1
  270.0 14.7 %all-to-all-start.2 = ((bf16[32,2,1664]{2,1,0:T(2,128)(2,1)}), bf16[32,2,1664]{2,1,0:T(2,128)(2,1)S(1)}, u32[]{:S(2)}, u32[]{:S(2)}) async-start(bf16[32,2,1664]{2,1,0:T(2,128)(2,1)} %broadcast_select_fusion.1), calls=%async_computation.3 | async-start | bytes 425984 | tf_op jit(solution)/shard_map/all_to_all | solution.py:94
  284.7 0.0 copy-start.3
  284.7 4.1 %fusion = bf16[1,1664,256]{2,1,0:T(8,128)(2,1)} fusion(bf16[1024,1664]{1,0:T(8,128)(2,1)} %all-gather.5.cloned.1.call-done, bf16[1024,256]{1,0:T(8,128)(2,1)S(1)} %fusion.3), kind=kOutput, calls=%fused_computation.7 | convolution fusion | flops 872841216 | bytes 4784128 | tf_op jit(solution)/shard_map/dot_general | solution.py:75
  288.8 0.0 copy-done.3
  288.8 2.1 fusion.1
  290.9 13.3 %all-to-all-done.2 = bf16[32,2,1664]{2,1,0:T(2,128)(2,1)S(1)} async-done(((bf16[32,2,1664]{2,1,0:T(2,128)(2,1)}), bf16[32,2,1664]{2,1,0:T(2,128)(2,1)S(1)}, u32[]{:S(2)}, u32[]{:S(2)}) %all-to-all-start.2) | async-done | bytes 213024 | tf_op jit(solution)/shard_map/all_to_all | solution.py:94
  304.2 0.1 reshape.237
  304.3 1.0 fusion.2
  (12 shorter events, 0.1 us)
Async XLA Ops:
  7.2 97.7 %copy-start = (bf16[1,1664,256]{2,1,0:T(8,128)(2,1)S(1)}, bf16[1,1664,256]{2,1,0:T(8,128)(2,1)}, u32[]{:S(2)}) copy-start(bf16[1,1664,256]{2,1,0:T(8,128)(2,1)} %param.11) | copy-start | bytes 2555908
  7.2 97.7 %all-gather.5.cloned.1.call-start = ((), (), s32[]{:S(2)}) async-start(), calls=%async_computation.5 | async-start | bytes 3620864 | tf_op jit(solution)/shard_map/all_gather | solution.py:63
  8.2 46.8 %copy-start.1 = (s32[16,32,1]{1,2,0:T(1,128)S(1)}, s32[16,32,1]{1,2,0:T(1,128)}, u32[]{:S(2)}) copy-start(s32[16,32,1]{1,2,0:T(1,128)} %param.14) | copy-start | bytes 6148
  8.2 47.5 %copy-start.2 = (f32[1,1,32]{2,1,0:T(1,128)S(1)}, f32[1,1,32]{2,1,0:T(1,128)}, u32[]{:S(2)}) copy-start(f32[1,1,32]{2,1,0:T(1,128)} %param.13) | copy-start | bytes 388
  50.1 24.5 %all-to-all-start = ((bf16[32,2,1664]{2,1,0:T(2,128)(2,1)}), bf16[32,2,1664]{2,1,0:T(2,128)(2,1)S(1)}, u32[]{:S(2)}, u32[]{:S(2)}) async-start(bf16[32,2,1664]{2,1,0:T(2,128)(2,1)} %reshape.234), calls=%async_computation | async-start | bytes 425984 | tf_op jit(solution)/shard_map/all_to_all | solution.py:46
  55.0 116.5 %all-gather.3.cloned.1.call-start = ((), (), s32[]{:S(2)}) async-start(), calls=%async_computation.4 | async-start | bytes 3620864 | tf_op jit(solution)/shard_map/all_gather | solution.py:64
  75.5 191.5 %reduce-scatter.2.cloned.1.call-start = ((), (), s32[]{:S(2)}) async-start(), calls=%async_computation.6 | async-start | bytes 1810432 | tf_op jit(solution)/shard_map/reduce_scatter | solution.py:83
  76.8 94.6 %copy-start.4 = (bf16[1,256,1664]{2,1,0:T(8,128)(2,1)S(1)}, bf16[1,256,1664]{2,1,0:T(8,128)(2,1)}, u32[]{:S(2)}) copy-start(bf16[1,256,1664]{2,1,0:T(8,128)(2,1)} %param.12) | copy-start | bytes 2555908
  270.0 34.3 %all-to-all-start.2 = ((bf16[32,2,1664]{2,1,0:T(2,128)(2,1)}), bf16[32,2,1664]{2,1,0:T(2,128)(2,1)S(1)}, u32[]{:S(2)}, u32[]{:S(2)}) async-start(bf16[32,2,1664]{2,1,0:T(2,128)(2,1)} %broadcast_select_fusion.1), calls=%async_computation.3 | async-start | bytes 425984 | tf_op jit(solution)/shard_map/all_to_all | solution.py:94
  284.7 4.1 %copy-start.3 = (bf16[1024,1664]{1,0:T(8,128)(2,1)S(1)}, bf16[1024,1664]{1,0:T(8,128)(2,1)}, u32[]{:S(2)}) copy-start(bf16[1024,1664]{1,0:T(8,128)(2,1)} %all-gather.3.cloned.1.call-done) | copy-start | bytes 10223620
Sparse Core Ops, SparseCore 0:
  49.5 55.3 all-gather.4
  108.5 62.8 all-gather.2
  179.0 87.9 reduce-scatter.1
where the time goes:
time: 312 us
  waiting for transfers between devices  212 us (68%)
  blocking collectives  36.1 us (12%)
  starting transfers between devices  19.7 us (6%)
  matrix products  15.7 us (5%)
  between operations  14 us (4%)
  local copies, waits for them, and re-layouts  11.2 us (4%)
  other arithmetic  3.6 us (1%)
    reduce_scatter x1, waiting for transfers between devices, on_device(): lax.psum_scatter(lax.dot_general(stash_rows, local_in, (((1,), (1,)), (()...  87.9 us
    all_gather x1, waiting for transfers between devices, on_device(): piece_grad = lax.all_gather(scaled_rows, 'dp', axis=0, tiled=True)  63.5 us
    all_to_all x1, blocking collectives, on_device(): lax.all_to_all(send_in, 'expert', split_axis=0, concat_axis=0, tiled=True)  36.1 us
    all_gather x1, waiting for transfers between devices, on_device(): piece_in = lax.all_gather(arrived_in, 'dp', axis=0, tiled=True)  28.1 us
    all_to_all x1, waiting for transfers between devices, on_device(): lax.all_to_all(send_grad, 'expert', split_axis=0, concat_axis=0, tiled=True)  18.8 us
    all_to_all x1, starting transfers between devices, on_device(): lax.all_to_all(returned, 'expert', split_axis=0, concat_axis=0, tiled=True)  14.7 us
    all_to_all x1, waiting for transfers between devices, on_device(): lax.all_to_all(returned, 'expert', split_axis=0, concat_axis=0, tiled=True)  13.3 us
  transfers between devices with their start and end apart: 5, of which 5 were waited for; matrix products, arithmetic and copies ran while one was open for 4% of the time, Pallas kernels for 0%

commit v1 on v0

--- a/solution.py
+++ b/solution.py
@@ -61,7 +61,13 @@
     padded_gates = jnp.sum(jnp.where(slot_hits, my_gates[None, :], 0.0), axis=1)
     scaled_rows = (padded_gates[:, None] * arrived_grad.astype(jnp.float32)).astype(jnp.bfloat16)
     piece_in = lax.all_gather(arrived_in, "dp", axis=0, tiled=True)
-    piece_grad = lax.all_gather(scaled_rows, "dp", axis=0, tiled=True)
+
+    def figure_number(x_local, axis_name):
+        v_next = jnp.stack([x_local] * jax.lax.axis_size(axis_name))
+        arr_now = jax.lax.all_to_all(v_next, axis_name, split_axis=0, concat_axis=0)
+        return jnp.concatenate(arr_now, 0)
+
+    piece_grad = figure_number(scaled_rows, "dp")
     preact = jnp.dot(piece_in, local_in, preferred_element_type=jnp.float32)
     gelu_value, gelu_slope = gelu_parts(preact)
     hidden = gelu_value.astype(jnp.bfloat16)

time: 312 us -> 279 us (0.89)
  waiting for transfers between devices: 212 us -> 168 us
  starting transfers between devices: 19.7 us -> 26.4 us
    all_gather x1 -> x0, waiting for transfers between devices: 63.5 us -> none  [on_device(): piece_grad = lax.all_gather(scaled_rows, 'dp', axis=0, tiled=True)]
    all_gather x1, waiting for transfers between devices: 28.1 us -> 56 us  [on_device(): piece_in = lax.all_gather(arrived_in, 'dp', axis=0, tiled=True)]
    all_to_all x0 -> x1, starting transfers between devices: none -> 6.8 us  [figure_number(): arr_now = jax.lax.all_to_all(v_next, axis_name, split_axis=0, concat_axis=0)]
    reduce_scatter x1, waiting for transfers between devices: 87.9 us -> 81.5 us  [on_device(): lax.psum_scatter(lax.dot_general(stash_rows, local_in, (((1,), (1,)), (()...]
  transfers between devices with their start and end apart: 5 -> 5, of which waited for: 5 -> 4; matrix products, arithmetic and copies ran while one was open for 4% -> 6% of each run, Pallas kernels for 0% -> 0%
where the time goes in v1:
time: 279 us; the launch traced here: 278 us
  waiting for transfers between devices  168 us (60%)
  blocking collectives  36.1 us (13%)
  starting transfers between devices  26.4 us (9%)
  matrix products  17.5 us (6%)
  between operations  14.3 us (5%)
  local copies, waits for them, and re-layouts  13.3 us (5%)
  other arithmetic  2.92 us (1%)
    reduce_scatter x1, waiting for transfers between devices, on_device(): lax.psum_scatter(lax.dot_general(stash_rows, local_in, (((1,), (1,)), (()...  81.5 us
    all_gather x1, waiting for transfers between devices, on_device(): piece_in = lax.all_gather(arrived_in, 'dp', axis=0, tiled=True)  56 us
    all_to_all x1, blocking collectives, on_device(): lax.all_to_all(send_in, 'expert', split_axis=0, concat_axis=0, tiled=True)  36.1 us
    all_to_all x1, waiting for transfers between devices, on_device(): lax.all_to_all(send_grad, 'expert', split_axis=0, concat_axis=0, tiled=True)  18.9 us
    all_to_all x1, starting transfers between devices, on_device(): lax.all_to_all(returned, 'expert', split_axis=0, concat_axis=0, tiled=True)  14.6 us
    all_to_all x1, waiting for transfers between devices, on_device(): lax.all_to_all(returned, 'expert', split_axis=0, concat_axis=0, tiled=True)  11.5 us
    all_to_all x1, starting transfers between devices, figure_number(): arr_now = jax.lax.all_to_all(v_next, axis_name, split_axis=0, concat_axis=0)  6.8 us
  transfers between devices with their start and end apart: 5, of which 4 were waited for; matrix products, arithmetic and copies ran while one was open for 6% of the time, Pallas kernels for 0%

profile of v1, /device:TPU:1, one launch (start us, length us, event | category | flops | bytes accessed | tf_op | source)
XLA Modules:
  0.0 278.5 jit_solution(2804326243128290287)
XLA Ops:
  7.2 0.0 copy-start
  7.2 0.0 all-gather.2.cloned.1.call-start
  7.2 0.8 copy.14
  8.1 0.1 eq.42
  8.2 0.0 copy-start.1
  8.2 0.0 copy-start.2
  8.2 2.0 gather_fusion.2
  10.2 2.0 gather_fusion.3
  12.2 0.1 broadcast_select_fusion.2
  12.3 0.1 reshape.248
  12.4 36.1 %all_to_all.20 = bf16[32,2,1664]{2,1,0:T(2,128)(2,1)S(1)} all-to-all(bf16[32,2,1664]{2,1,0:T(2,128)(2,1)S(1)} %reshape.248), channel_id=1, replica_groups=mesh['expert'=32,'dp'=16] {'expert'}, dimensions={0} | all-to-all | bytes 425984 | tf_op jit(solution)/shard_map/all_to_all | solution.py:45
  48.6 0.8 reshape.249
  49.3 0.0 all-gather.2.cloned.1.call-update
  49.3 0.8 reshape.246
  50.1 4.9 %all-to-all-start = ((bf16[32,2,1664]{2,1,0:T(2,128)(2,1)}), bf16[32,2,1664]{2,1,0:T(2,128)(2,1)S(1)}, u32[]{:S(2)}, u32[]{:S(2)}) async-start(bf16[32,2,1664]{2,1,0:T(2,128)(2,1)} %reshape.246), calls=%async_computation | async-start | bytes 425984 | tf_op jit(solution)/shard_map/all_to_all | solution.py:46
  55.0 0.0 copy-done.1
  55.0 0.1 copy.15
  55.1 0.1 reduce-window.8
  55.2 0.1 reduce
  55.3 0.1 broadcast_clamp_fusion
  55.4 0.1 add.147
  55.5 0.1 iota_compare_fusion.5
  55.5 0.1 lt.83
  55.7 0.0 copy-done.2
  55.7 0.1 select_reduce_fusion.1
  55.8 18.9 %all-to-all-done = bf16[32,2,1664]{2,1,0:T(2,128)(2,1)S(1)} async-done(((bf16[32,2,1664]{2,1,0:T(2,128)(2,1)}), bf16[32,2,1664]{2,1,0:T(2,128)(2,1)S(1)}, u32[]{:S(2)}, u32[]{:S(2)}) %all-to-all-start) | async-done | bytes 213024 | tf_op jit(solution)/shard_map/all_to_all | solution.py:46
  74.6 0.1 reshape.251
  74.7 0.1 multiply_convert_fusion.2
  74.8 2.1 stack.2
  76.9 6.8 %all-to-all-start.1 = ((bf16[16,64,1664]{2,1,0:T(8,128)(2,1)}), bf16[16,64,1664]{2,1,0:T(8,128)(2,1)}, u32[]{:S(2)}, u32[]{:S(2)}) async-start(bf16[16,64,1664]{2,1,0:T(8,128)(2,1)} %stack.2), calls=%async_computation.1 | async-start | bytes 6815744 | tf_op jit(solution)/shard_map/all_to_all | solution.py:67
  83.7 0.0 reduce-scatter.2.cloned.1.call-start
  83.8 0.2 reduce_window_sum.18
  84.0 0.3 convert_reduce_fusion
  84.3 0.5 select_reduce_fusion
  84.8 0.1 subtract_add_fusion
  84.9 0.1 add.152
  85.0 0.1 add.144
  85.1 0.0 copy-start.3
  85.1 56.0 %all-gather.2.cloned.1.call-done = bf16[1024,1664]{1,0:T(8,128)(2,1)} async-done(((bf16[64,1664]{1,0:T(8,128)(2,1)}), bf16[1024,1664]{1,0:T(8,128)(2,1)}) %all-gather.2.cloned.1.call-update) | async-done | bytes 3407888 | tf_op jit(solution)/shard_map/all_gather | solution.py:63
  141.1 0.0 copy-done
  141.1 3.1 %fusion.10 = f32[1024,256]{1,0:T(8,128)S(1)} fusion(bf16[1024,1664]{1,0:T(8,128)(2,1)} %all-gather.2.cloned.1.call-done, bf16[1,1664,256]{2,1,0:T(8,128)(2,1)S(1)} %copy-done), kind=kOutput, calls=%fused_computation.22 | convolution fusion | flops 872415232 | bytes 5308416 | tf_op jit(solution)/shard_map/dot_general | solution.py:71
  144.2 0.0 all-to-all-done.1
  144.2 0.0 copy-done.3
  144.2 3.5 %fusion.3 = bf16[1024,256]{1,0:T(8,128)(2,1)S(1)} fusion(bf16[1024,1664]{1,0:T(8,128)(2,1)} %bitcast.5, f32[1024,256]{1,0:T(8,128)S(1)} %fusion.10, bf16[1,256,1664]{2,1,0:T(8,128)(2,1)S(1)} %copy-done.3), kind=kOutput, calls=%fused_computation.14 | convolution fusion | flops 877395968 | bytes 5832704 | tf_op jit(solution)/shard_map/dot_general | solution.py:74
  147.7 2.0 gather_fusion
  149.6 1.9 convolution_convert_fusion
  151.5 0.0 reduce-scatter.2.cloned.1.call-update
  151.6 0.1 min.12
  151.7 0.1 compare_and_fusion
  151.8 81.5 %reduce-scatter.2.cloned.1.call-done = bf16[32,1664]{1,0:T(8,128)(2,1)} async-done(((bf16[512,1664]{1,0:T(8,128)(2,1)}), bf16[32,1664]{1,0:T(8,128)(2,1)}) %reduce-scatter.2.cloned.1.call-update) | async-done | bytes 106512 | tf_op jit(solution)/shard_map/reduce_scatter | solution.py:89
  233.3 1.8 gather_fusion.1
  235.1 0.1 gather.15
  235.2 1.1 broadcast_select_fusion.1
  236.3 14.6 %all-to-all-start.3 = ((bf16[32,2,1664]{2,1,0:T(2,128)(2,1)}), bf16[32,2,1664]{2,1,0:T(2,128)(2,1)S(1)}, u32[]{:S(2)}, u32[]{:S(2)}) async-start(bf16[32,2,1664]{2,1,0:T(2,128)(2,1)} %broadcast_select_fusion.1), calls=%async_computation.4 | async-start | bytes 425984 | tf_op jit(solution)/shard_map/all_to_all | solution.py:100
  251.0 4.0 %fusion = bf16[1,1664,256]{2,1,0:T(8,128)(2,1)} fusion(bf16[1024,1664]{1,0:T(8,128)(2,1)} %all-gather.2.cloned.1.call-done, bf16[1024,256]{1,0:T(8,128)(2,1)S(1)} %fusion.3), kind=kOutput, calls=%fused_computation.7 | convolution fusion | flops 872841216 | bytes 4784128 | tf_op jit(solution)/shard_map/dot_general | solution.py:81
  254.9 4.1 %fusion.1 = bf16[1,256,1664]{2,1,0:T(8,128)(2,1)} fusion(bf16[1024,1664]{1,0:T(8,128)(2,1)} %bitcast.5, f32[1024,256]{1,0:T(8,128)S(1)} %fusion.10), kind=kOutput, calls=%fused_computation.8 | convolution fusion | flops 875200512 | bytes 5308416 | tf_op jit(solution)/shard_map/dot_general | solution.py:78
  259.0 11.5 %all-to-all-done.3 = bf16[32,2,1664]{2,1,0:T(2,128)(2,1)S(1)} async-done(((bf16[32,2,1664]{2,1,0:T(2,128)(2,1)}), bf16[32,2,1664]{2,1,0:T(2,128)(2,1)S(1)}, u32[]{:S(2)}, u32[]{:S(2)}) %all-to-all-start.3) | async-done | bytes 213024 | tf_op jit(solution)/shard_map/all_to_all | solution.py:100
  270.5 0.1 reshape.250
  270.6 1.0 fusion.2
  (12 shorter events, 0.1 us)
Async XLA Ops:
  7.2 133.9 %copy-start = (bf16[1,1664,256]{2,1,0:T(8,128)(2,1)S(1)}, bf16[1,1664,256]{2,1,0:T(8,128)(2,1)}, u32[]{:S(2)}) copy-start(bf16[1,1664,256]{2,1,0:T(8,128)(2,1)} %param.11) | copy-start | bytes 2555908
  7.2 133.9 %all-gather.2.cloned.1.call-start = ((), (), s32[]{:S(2)}) async-start(), calls=%async_computation.5 | async-start | bytes 3620864 | tf_op jit(solution)/shard_map/all_gather | solution.py:63
  8.2 46.8 %copy-start.1 = (s32[16,32,1]{1,2,0:T(1,128)S(1)}, s32[16,32,1]{1,2,0:T(1,128)}, u32[]{:S(2)}) copy-start(s32[16,32,1]{1,2,0:T(1,128)} %param.14) | copy-start | bytes 6148
  8.2 47.5 %copy-start.2 = (f32[1,1,32]{2,1,0:T(1,128)S(1)}, f32[1,1,32]{2,1,0:T(1,128)}, u32[]{:S(2)}) copy-start(f32[1,1,32]{2,1,0:T(1,128)} %param.13) | copy-start | bytes 388
  50.1 24.5 %all-to-all-start = ((bf16[32,2,1664]{2,1,0:T(2,128)(2,1)}), bf16[32,2,1664]{2,1,0:T(2,128)(2,1)S(1)}, u32[]{:S(2)}, u32[]{:S(2)}) async-start(bf16[32,2,1664]{2,1,0:T(2,128)(2,1)} %reshape.246), calls=%async_computation | async-start | bytes 425984 | tf_op jit(solution)/shard_map/all_to_all | solution.py:46
  76.9 67.2 %all-to-all-start.1 = ((bf16[16,64,1664]{2,1,0:T(8,128)(2,1)}), bf16[16,64,1664]{2,1,0:T(8,128)(2,1)}, u32[]{:S(2)}, u32[]{:S(2)}) async-start(bf16[16,64,1664]{2,1,0:T(8,128)(2,1)} %stack.2), calls=%async_computation.1 | async-start | bytes 6815744 | tf_op jit(solution)/shard_map/all_to_all | solution.py:67
  83.7 149.6 %reduce-scatter.2.cloned.1.call-start = ((), (), s32[]{:S(2)}) async-start(), calls=%async_computation.6 | async-start | bytes 1810432 | tf_op jit(solution)/shard_map/reduce_scatter | solution.py:89
  85.1 59.1 %copy-start.3 = (bf16[1,256,1664]{2,1,0:T(8,128)(2,1)S(1)}, bf16[1,256,1664]{2,1,0:T(8,128)(2,1)}, u32[]{:S(2)}) copy-start(bf16[1,256,1664]{2,1,0:T(8,128)(2,1)} %param.12) | copy-start | bytes 2555908
  236.3 34.2 %all-to-all-start.3 = ((bf16[32,2,1664]{2,1,0:T(2,128)(2,1)}), bf16[32,2,1664]{2,1,0:T(2,128)(2,1)S(1)}, u32[]{:S(2)}, u32[]{:S(2)}) async-start(bf16[32,2,1664]{2,1,0:T(2,128)(2,1)} %broadcast_select_fusion.1), calls=%async_computation.4 | async-start | bytes 425984 | tf_op jit(solution)/shard_map/all_to_all | solution.py:100
Sparse Core Ops, SparseCore 0:
  49.5 91.5 all-gather.1
  151.7 81.5 reduce-scatter.1
